TPU v7x, 32 devices: a whole 2x2x4 slice. The times are simulated.
32 devices in a mesh: depth: 4 (over x, core), rows: 8 (over z, y).
Axes of the slice: x: 2, y: 2, z: 4, core: 2. Of those that a mesh axis runs over, the one named last changes fastest.
Arguments:
- volume: bfloat16 [4, 64, 256, 4096], P(None, 'depth', 'rows')
- shear_rows: int32 [64], P('depth'), may hold values from -8 to 8, as said below
- shear_cols: int32 [64], P('depth'), may hold values from -8 to 8, as said below
- warp_cols: int32 [256], replicated, may hold values from -8 to 8, as said below
- warp_rows: int32 [4096], P('depth'), may hold values from -8 to 8, as said below
Outputs:
- final_image: float32 [4, 256, 4096], P(None, 'rows', 'depth')
Inputs may be any that keep to these rules, and one draw needn't show every extreme that they name: `shear_rows`: both -8 and 8 occur. `shear_cols`: both -8 and 8 occur. `warp_cols`: both -8 and 8 occur. `warp_rows`: both -8 and 8 occur.
All inputs are finite; a program needn't handle non-finite values.
Results may differ from a plain program's by a relative error of at most 0.0017.
Values may be sent and summed in bfloat16 or wider, within the bound.
A program may use at most 192 MiB of HBM per device.

v0:
```python
import functools

import jax
import jax.numpy as jnp
from jax import lax
from jax.experimental import pallas as pl
from jax.experimental.pallas import tpu as pltpu
from jax.sharding import PartitionSpec as P

SHIFT = 8
RIM = SHIFT + 1
GROUP = 16
EDGE = 16
LANES = 128
LEAD = 16
CHUNK = 512
BLOCK = 8
SLOT = 10
AHEAD = 4
GHOST_LAG = 2
MERGE_LAG = 4
BF = jnp.bfloat16
F32 = jnp.float32
MESH = pl.DeviceIdType.MESH


def weight_of(offset):
    return jnp.where(offset == 0, 0.5, jnp.where(jnp.abs(offset) == 1, 0.25, 0.0)).astype(F32)


def iota(shape, dim):
    return lax.broadcasted_iota(jnp.int32, shape, dim)


def slab_kernel(
    sizes, row_s, col_s, warp_s, turn_ref, vol_hbm,
    out_ref,
    vol, a_send, a_recv, t_send, t_recv, c_send, c_recv, spread, own_w, colour_w, w_col, unpack, collect,
    pick_a, pick_t, band_a, band_c, trans, t_all, ghost, acc, outb, parts, wide_ref, f_send, f_recv,
    load_sem, a_ss, a_rs, t_ss, t_rs, c_ss, c_rs, s_part, r_part, f_ss, f_rs,
):
    depth, n_rows = sizes
    chunks, channels, slab, rows, _ = vol.shape
    colours = channels - 1
    high = a_send.shape[2]
    cols = chunks * CHUNK
    tile = cols // depth
    per = CHUNK // LANES
    per_tile = tile // LANES
    pieces = tile // CHUNK
    flat = channels * rows
    tint = colours * rows
    step = BLOCK * rows
    me = lax.axis_index("depth")
    row = lax.axis_index("rows")
    has = (row > 0, row < n_rows - 1)
    got = (row < n_rows - 1, row > 0)
    target = (jnp.maximum(row - 1, 0), jnp.minimum(row + 1, n_rows - 1))

    def load_alpha(i):
        at = pl.ds(pl.multiple_of(i * CHUNK, CHUNK), CHUNK)
        return pltpu.make_async_copy(vol_hbm.at[colours, :, :, at], vol.at[i, colours], load_sem.at[0, i])

    def load_colour(i):
        at = pl.ds(pl.multiple_of(i * CHUNK, CHUNK), CHUNK)
        return pltpu.make_async_copy(
            vol_hbm.at[pl.ds(0, colours), :, :, at], vol.at[i, pl.ds(0, colours)], load_sem.at[1, i]
        )

    order = [chunks - 1] + list(range(chunks - 1))
    for i in order:
        load_alpha(i).start()
    for i in order:
        load_colour(i).start()

    barrier = pltpu.get_barrier_semaphore()
    for r in (lax.rem(row + 1, n_rows), lax.rem(row + n_rows - 1, n_rows)):
        pl.semaphore_signal(barrier, inc=1, device_id=(me, r), device_id_type=MESH)
    for m in range(1, depth):
        pl.semaphore_signal(barrier, inc=1, device_id=(lax.rem(me + m, depth), row), device_id_type=MESH)
    pl.semaphore_wait(barrier, depth + 1)

    def message(kind, way, i):
        source, dest, ss, rs = kind
        return pltpu.make_async_remote_copy(
            source.at[way, i], dest.at[way, i], ss.at[way, i], rs.at[way, i],
            device_id=(me, target[way]), device_id_type=MESH,
        )

    def lead_message(way):
        part = pl.ds(0, LANES)
        return pltpu.make_async_remote_copy(
            a_send.at[way, chunks, :, part], a_recv.at[way, chunks, :, part],
            a_ss.at[way, chunks], a_rs.at[way, chunks],
            device_id=(me, target[way]), device_id_type=MESH,
        )

    kind_a = (a_send, a_recv, a_ss, a_rs)
    kind_t = (t_send, t_recv, t_ss, t_rs)
    kind_c = (c_send, c_recv, c_ss, c_rs)
    kind_f = (f_send, f_recv, f_ss, f_rs)

    def start(kind, i):
        for way in range(2):
            @pl.when(has[way])
            def _():
                message(kind, way, i).start()

    def arrived(kind, i):
        for way in range(2):
            @pl.when(got[way])
            def _():
                message(kind, way, i).wait_recv()

    def sent(kind, i):
        for way in range(2):
            @pl.when(has[way])
            def _():
                message(kind, way, i).wait_send()

    def counts(k):
        return jnp.maximum(0, row_s[k] + 1), jnp.maximum(0, 1 - row_s[k])

    def tables(k, carry):
        ou, od, at, slots, side = carry
        n_up, n_dn = counts(k)
        u = iota((1, slab * EDGE), 1) - k * EDGE
        v = u - (EDGE - n_dn)
        up = jnp.where((u >= 0) & (u < n_up), ou + u, at[0])
        dn = jnp.where((v >= 0) & (u < EDGE), od + v, at[1])
        u = iota((1, slab * rows), 1) - k * rows
        v = u - (rows - n_up)
        north = jnp.where((u >= 0) & (u < n_dn), od + u, slots[0])
        south = jnp.where((v >= 0) & (u < rows), ou + v, slots[1])
        side = jnp.where((u >= 0) & (u < rows), row_s[k], side)
        return ou + n_up, od + n_dn, (up, dn), (north, south), side

    none = jnp.full((1, slab * EDGE), -1, jnp.int32)
    nowhere = jnp.full((1, slab * rows), -1, jnp.int32)
    zero = jnp.int32(0)
    table = lax.fori_loop(0, slab, tables, (zero, zero, (none, none), (nowhere, nowhere), nowhere))
    _, _, at_rows, slot_rows, shift_of = table

    firsts = (0, rows - EDGE)
    for way in range(2):
        slots = at_rows[way]
        pick_a[way] = (iota((high, slab * EDGE), 0) == slots).astype(F32).astype(BF)

    def pack(i, way, at):
        first = firsts[way]
        source = vol[i, colours, :, first : first + EDGE, at : CHUNK]
        source = source.reshape(slab * EDGE, CHUNK - at)
        return jnp.dot(pick_a[way], source, preferred_element_type=F32).astype(BF)

    load_alpha(chunks - 1).wait()
    for way in range(2):
        a_send[way, chunks, :, :LANES] = pack(chunks - 1, way, CHUNK - LANES)

    @pl.loop(0, chunks)
    def _(i):
        @pl.when(i < chunks - 1)
        def _():
            load_alpha(i).wait()

        for way in range(2):
            a_send[way, i] = pack(i, way, 0)

        @pl.when(i == 0)
        def _():
            for way in range(2):
                @pl.when(has[way])
                def _():
                    lead_message(way).start()

        @pl.when((i > 0) & (i <= AHEAD))
        def _():
            start(kind_a, i - 1)

    for way in range(2):
        @pl.when(jnp.logical_not(got[way]))
        def _():
            a_recv[way] = jnp.zeros(a_recv.shape[1:], BF)
            t_recv[way] = jnp.zeros(t_recv.shape[1:], BF)
            c_recv[way] = jnp.zeros(c_recv.shape[1:], BF)
            f_recv[way] = jnp.zeros(f_recv.shape[1:], BF)

    lane = iota((high, slab * rows), 0)
    for way in range(2):
        slots = slot_rows[way]
        pick_t[way * high : (way + 1) * high] = (lane == slots).astype(F32).astype(BF)
    shape = (2 * rows, slab * rows)
    m = iota(shape, 0)
    j = iota(shape, 1)
    s = shift_of
    e = (j % rows) % SLOT
    side = jnp.where(s > 0, 0, jnp.where(s < 0, 1, jnp.where(e >= SHIFT // 2 + 1, 0, 1)))
    collect[...] = (((m % rows) + rows * (m // rows)) == ((j % rows) + rows * side)).astype(F32).astype(BF)

    def build(k, carry):
        ou, od = carry
        s = row_s[k]
        n_up, n_dn = counts(k)
        mine = pl.ds(pl.multiple_of(k * rows, rows), rows)
        y = iota((rows, high), 0)
        slot = iota((rows, high), 1)
        u = slot - ou
        keep = (u >= 0) & (u < n_up)
        spread[mine, :high] = jnp.where(keep, weight_of(rows + u - y - s), 0.0).astype(BF)
        v = slot - od
        keep = (v >= 0) & (v < n_dn)
        spread[mine, high:] = jnp.where(keep, weight_of(v - n_dn - y - s), 0.0).astype(BF)
        e = jnp.where(y < colours * SLOT, y % SLOT, -1 - 2 * rows)
        e = jnp.where(e > SHIFT, -1 - 2 * rows, e)
        hit = (v == e) & (v < n_dn) & (v >= 0)
        unpack[mine, :high] = hit.astype(F32).astype(BF)
        hit = (u == e - SHIFT + s) & (u < n_up) & (u >= 0)
        unpack[mine, high:] = hit.astype(F32).astype(BF)
        y = iota((rows, step), 0)
        j = iota((rows, step), 1)
        own_w[mine] = jnp.where(
            (j // rows) == lax.rem(k, BLOCK), weight_of((j % rows) - y - s), 0.0
        ).astype(BF)
        m = iota((flat, tint), 0)
        j = iota((flat, tint), 1)
        e = (m - tint) % SLOT
        north = jnp.where(s > 0, 1, jnp.where(s < 0, 0, jnp.where(e >= SHIFT // 2 + 1, 1, 0)))
        y = jnp.where(m < tint, m % rows, jnp.where(north > 0, e - RIM, rows + e))
        c = jnp.where(m < tint, m // rows, (m - tint) // SLOT)
        same = c == (j // rows)
        colour_w[k] = jnp.where(same, weight_of((j % rows) - y - s), 0.0).astype(BF)
        shape = (2 * LANES, LANES)
        m = iota(shape, 0)
        n = iota(shape, 1)
        w = weight_of(m - n - (LANES - LEAD) - col_s[k])
        w_col[0, k] = w.astype(BF)
        w_col[1, k] = jnp.where(jnp.where(m < LANES, 0, 1) == jnp.where(n < LEAD, 0, 1), w, 0.0).astype(BF)
        return ou + n_up, od + n_dn

    lax.fori_loop(0, slab, build, (zero, zero))

    def alpha_rows(i, at, to, width):
        halo = jnp.concatenate([a_recv[way, i, :, :width] for way in range(2)], 0)
        source = i if at == 0 else chunks - 1
        for b in range(slab // BLOCK):
            part = slice(b * step, (b + 1) * step)
            own = vol[source, colours, b * BLOCK : (b + 1) * BLOCK, :, at : at + width]
            own = own.reshape(step, width)
            total = jnp.dot(own_w[part], own, preferred_element_type=F32)
            total = total + jnp.dot(spread[part], halo, preferred_element_type=F32)
            band_a[part, to : to + width] = total.astype(BF)

    def colour_rows(i, k, at, width):
        opacity = vol[i, colours, k, :, at : at + width]
        own = [vol[i, c, k, :, at : at + width] * opacity for c in range(colours)]
        return jnp.dot(colour_w[k], jnp.concatenate(own, 0), preferred_element_type=F32).astype(BF)

    for way in range(2):
        @pl.when(got[way])
        def _():
            lead_message(way).wait_recv()

    alpha_rows(chunks, CHUNK - LANES, CHUNK, LANES)
    load_colour(chunks - 1).wait()

    @pl.loop(0, slab)
    def _(k):
        band_c[k, :, CHUNK:] = colour_rows(chunks - 1, k, CHUNK - LANES, LANES)

    def composite(i):
        arrived(kind_a, i)

        @pl.when(i < chunks - 1)
        def _():
            load_colour(i).wait()

        band_a[:, :LANES] = band_a[:, CHUNK:]
        alpha_rows(i, 0, LANES, CHUNK)
        trans[...] = jnp.ones_like(trans)
        acc[i] = jnp.zeros(acc.shape[1:], F32)
        lead = jnp.where(i == 0, 1, 0)

        @pl.loop(0, slab, unroll=4)
        def _(k):
            band_c[k, :, :LANES] = band_c[k, :, CHUNK:]
            band_c[k, :, LANES:] = colour_rows(i, k, 0, CHUNK)

        @pl.loop(0, slab, unroll=4)
        def _(k):
            mine = pl.ds(pl.multiple_of(k * rows, rows), rows)

            def window(w):
                at = slice(w * LANES, (w + 2) * LANES)
                return [band_a[mine, at], band_c[k, :, at]]

            first = jnp.dot(
                jnp.concatenate(window(0), 0), w_col[lead, k], preferred_element_type=F32
            )
            others = sum([window(w) for w in range(1, per)], [])
            rest = jnp.dot(jnp.concatenate(others, 0), w_col[0, k], preferred_element_type=F32)
            tall = rows + flat
            for w in range(per):
                sheared = first if w == 0 else rest[(w - 1) * tall : w * tall]
                at = slice(w * LANES, (w + 1) * LANES)
                t = trans[:, at]
                for c in range(colours):
                    acc[i, c * rows : (c + 1) * rows, at] += t * sheared[(c + 1) * rows : (c + 2) * rows]
                ghost[i, mine, at] = sheared[flat:].astype(BF)
                t_all[mine, at] = t.astype(BF)
                trans[:, at] = t - t * sheared[:rows]

        acc[i, tint:] = 1.0 - trans[...]
        picked = jnp.dot(pick_t[...], t_all[...], preferred_element_type=F32).astype(BF)
        t_send[0, i] = picked[:high]
        t_send[1, i] = picked[high:]

    def ghosts(i):
        arrived(kind_t, i)
        seen = jnp.concatenate([t_recv[0, i], t_recv[1, i]], 0)
        total = None
        for b in range(slab // BLOCK):
            part = slice(b * step, (b + 1) * step)
            t = jnp.dot(unpack[part], seen, preferred_element_type=F32)
            seen_colour = (t * ghost[i, part].astype(F32)).astype(BF)
            value = jnp.dot(collect[:, part], seen_colour, preferred_element_type=F32)
            total = value if total is None else total + value
        total = total.astype(BF)
        c_send[0, i] = total[:rows]
        c_send[1, i] = total[rows:]

    def merge(i):
        arrived(kind_c, i)
        m = iota((tint, 2 * rows), 0)
        j = iota((tint, 2 * rows), 1)
        e = (j % rows) % SLOT
        y = jnp.where(j < rows, rows - RIM + e, e)
        there = (m // rows == (j % rows) // SLOT) & (m % rows == y) & (e <= SHIFT)
        place = there.astype(F32).astype(BF)
        both = jnp.concatenate([c_recv[0, i], c_recv[1, i]], 0)
        more = jnp.dot(place, both, preferred_element_type=F32)
        image = jnp.concatenate([acc[i, :tint] + more, acc[i, tint:]], 0)
        for w in range(per):
            outb[i * per + w] = image[:, w * LANES : (w + 1) * LANES].astype(BF)

        @pl.when(i == 0)
        def _():
            piece = image[:, :LANES]
            n = iota((flat, LANES), 1)
            outb[chunks * per] = jnp.where(n < LEAD, piece, 0.0).astype(BF)
            outb[0] = jnp.where(n < LEAD, 0.0, piece).astype(BF)

    def part_copy(i, source, count, owner, at, margin):
        return pltpu.make_async_remote_copy(
            outb.at[pl.ds(source, count)],
            parts.at[me, pl.ds(at, count)],
            s_part.at[margin, i],
            r_part.at[me, pieces if margin else lax.rem(i, pieces)],
            device_id=(owner, row),
            device_id_type=MESH,
        )

    def deliver(i, act, keep):
        owner = i // pieces
        at = lax.rem(i, pieces) * per

        @pl.when(owner != me)
        def _():
            act(part_copy(i, i * per, per, owner, at, 0))

        if keep:
            @pl.when(owner == me)
            def _():
                parts[me, pl.ds(at, per)] = outb[pl.ds(i * per, per)]

        margin = lax.rem(i, pieces) == 0
        left = lax.rem(owner + depth - 1, depth)
        source = jnp.where(i == 0, chunks * per, i * per)

        @pl.when(margin & (left != me))
        def _():
            act(part_copy(i, source, 1, left, per_tile, 1))

        if keep:
            @pl.when(margin & (left == me))
            def _():
                parts[me, per_tile] = outb[source]

    @pl.loop(0, chunks + MERGE_LAG)
    def _(i):
        @pl.when(i < chunks)
        def _():
            composite(i)

        @pl.when((i >= GHOST_LAG) & (i < chunks + GHOST_LAG))
        def _():
            ghosts(i - GHOST_LAG)

        @pl.when(i < chunks)
        def _():
            start(kind_t, i)

        @pl.when(i + AHEAD < chunks)
        def _():
            start(kind_a, i + AHEAD)

        @pl.when(i > MERGE_LAG)
        def _():
            deliver(i - MERGE_LAG - 1, lambda copy: copy.start(), True)

        @pl.when(i >= MERGE_LAG)
        def _():
            merge(i - MERGE_LAG)

        @pl.when((i >= GHOST_LAG) & (i < chunks + GHOST_LAG))
        def _():
            start(kind_c, i - GHOST_LAG)

    deliver(jnp.int32(chunks - 1), lambda copy: copy.start(), True)

    for d in range(depth):
        @pl.when(me != d)
        def _():
            for p in range(pieces + 1):
                count = per if p < pieces else 1
                pltpu.make_async_remote_copy(
                    outb.at[pl.ds(0, count)],
                    parts.at[d, pl.ds(p * per, count)],
                    s_part.at[0, 0],
                    r_part.at[d, p],
                    device_id=(me, row),
                    device_id_type=MESH,
                ).wait_recv()

    for w in range(per_tile + 1):
        image = parts[0, w].astype(F32)
        image = image.reshape(channels, rows, LANES)
        for d in range(1, depth):
            back = parts[d, w].astype(F32).reshape(channels, rows, LANES)
            image = image + (1.0 - image[channels - 1 :]) * back
        wide_ref[:, w * LANES : (w + 1) * LANES] = image.reshape(flat, LANES)

    amount = jnp.zeros((rows, LANES), jnp.int32)
    for y in range(rows):
        amount = jnp.where(iota((rows, LANES), 0) == y, warp_s[row * rows + y] + SHIFT, amount)
    amount = jnp.concatenate([amount] * ((CHUNK + LANES) // LANES), 1)
    packed = f_send.shape[2]
    m = iota((packed, flat), 0)
    j = iota((packed, flat), 1)
    picks = []
    for first in (0, rows - RIM):
        there = (m // RIM == j // rows) & (m % RIM + first == j % rows)
        picks.append(there.astype(F32).astype(BF))
    width = CHUNK + LANES
    for h in range(pieces):
        lines = []
        for c in range(channels):
            line = wide_ref[c * rows : (c + 1) * rows, h * CHUNK : h * CHUNK + width]
            line = 0.5 * line + 0.25 * (pltpu.roll(line, 1, 1) + pltpu.roll(line, width - 1, 1))
            line = pltpu.roll(line, width - (LEAD - SHIFT), 1)
            for bit in (1, 2, 4, 8, 16):
                line = jnp.where((amount & bit) != 0, pltpu.roll(line, width - bit, 1), line)
            lines.append(line[:, :CHUNK])
        across = jnp.concatenate(lines, 0)
        wide_ref[:, h * CHUNK : (h + 1) * CHUNK] = across
        across = across.astype(BF)
        for way in range(2):
            f_send[way, h] = jnp.dot(picks[way], across, preferred_element_type=F32).astype(BF)
        if h > 0:
            start(kind_f, h - 1)
    start(kind_f, pieces - 1)

    half = rows // 2
    m = iota((flat, 2 * packed), 0)
    j = iota((flat, 2 * packed), 1)
    a = m % rows
    e = jnp.where(j < packed, a - half + RIM, a - half)
    slot = jnp.where(j < packed, j, j - packed)
    wanted = jnp.where(a < half, jnp.where(j < packed, e, -1), jnp.where(j < packed, -1, e))
    place = (slot // RIM == m // rows) & (slot % RIM == wanted)
    place = place.astype(F32).astype(BF)
    for h in range(pieces):
        arrived(kind_f, h)
        at = slice(h * CHUNK, (h + 1) * CHUNK)
        rim = jnp.concatenate([f_recv[1, h], f_recv[0, h]], 0)
        rim = jnp.dot(place, rim, preferred_element_type=F32)
        turn = turn_ref[:, at] + SHIFT
        for c in range(channels):
            low = rim[c * rows : c * rows + half]
            high_rows = rim[c * rows + half : (c + 1) * rows]
            ext = jnp.concatenate([low, wide_ref[c * rows : (c + 1) * rows, at], high_rows], 0)
            tall = ext.shape[0]
            ext = 0.5 * ext + 0.25 * (pltpu.roll(ext, 1, 0) + pltpu.roll(ext, tall - 1, 0))
            line = ext[half - SHIFT :]
            keep = rows + 2 * SHIFT
            line = jnp.where((turn & 8) != 0, line[8 : 8 + keep], line[:keep])
            far = jnp.concatenate([line[16 : 16 + rows], line[16 + rows - 8 : 16 + rows]], 0)
            line = jnp.where((turn & 16) != 0, far, line[: rows + 8])
            tall = rows + 8
            for bit in (4, 2, 1):
                line = jnp.where((turn & bit) != 0, pltpu.roll(line, tall - bit, 0), line)
            out_ref[c, :, at] = line[:rows]

    for way in range(2):
        @pl.when(has[way])
        def _():
            lead_message(way).wait_send()

    @pl.loop(0, chunks)
    def _(i):
        for kind in (kind_a, kind_t, kind_c):
            sent(kind, i)
        deliver(i, lambda copy: copy.wait_send(), False)

    for h in range(pieces):
        sent(kind_f, h)


def slab_stage(high, number, depth, n_rows, volume, scalars, turn):
    channels, slab, rows, cols = volume.shape
    chunks = cols // CHUNK
    per = CHUNK // LANES
    tile = cols // depth
    flat = channels * rows
    tint = flat - rows
    pieces = tile // CHUNK
    smem = pl.BlockSpec(memory_space=pltpu.SMEM)
    vmem = pl.BlockSpec(memory_space=pltpu.VMEM)
    packed = -(-channels * RIM // EDGE) * EDGE
    dma = pltpu.SemaphoreType.DMA
    return pl.pallas_call(
        functools.partial(slab_kernel, (depth, n_rows)),
        in_specs=[smem] * 3 + [vmem] + [pl.BlockSpec(memory_space=pl.ANY)],
        out_specs=vmem,
        out_shape=jax.ShapeDtypeStruct((channels, rows, tile), F32),
        scratch_shapes=[
            pltpu.VMEM((chunks, channels, slab, rows, CHUNK), BF),
            pltpu.VMEM((2, chunks + 1, high, CHUNK), BF),
            pltpu.VMEM((2, chunks + 1, high, CHUNK), BF),
            pltpu.VMEM((2, chunks, high, CHUNK), BF),
            pltpu.VMEM((2, chunks, high, CHUNK), BF),
            pltpu.VMEM((2, chunks, rows, CHUNK), BF),
            pltpu.VMEM((2, chunks, rows, CHUNK), BF),
            pltpu.VMEM((slab * rows, 2 * high), BF),
            pltpu.VMEM((slab * rows, BLOCK * rows), BF),
            pltpu.VMEM((slab, flat, tint), BF),
            pltpu.VMEM((2, slab, 2 * LANES, LANES), BF),
            pltpu.VMEM((slab * rows, 2 * high), BF),
            pltpu.VMEM((2 * rows, slab * rows), BF),
            pltpu.VMEM((2, high, slab * EDGE), BF),
            pltpu.VMEM((2 * high, slab * rows), BF),
            pltpu.VMEM((slab * rows, LANES + CHUNK), BF),
            pltpu.VMEM((slab, flat, LANES + CHUNK), BF),
            pltpu.VMEM((rows, CHUNK), F32),
            pltpu.VMEM((slab * rows, CHUNK), BF),
            pltpu.VMEM((chunks, slab * rows, CHUNK), BF),
            pltpu.VMEM((chunks, flat, CHUNK), F32),
            pltpu.VMEM((chunks * per + 1, flat, LANES), BF),
            pltpu.VMEM((depth, tile // LANES + 1, flat, LANES), BF),
            pltpu.VMEM((flat, tile + LANES), F32),
            pltpu.VMEM((2, pieces, packed, CHUNK), BF),
            pltpu.VMEM((2, pieces, packed, CHUNK), BF),
            dma((2, chunks)),
            dma((2, chunks + 1)),
            dma((2, chunks + 1)),
            dma((2, chunks)),
            dma((2, chunks)),
            dma((2, chunks)),
            dma((2, chunks)),
            dma((2, chunks)),
            dma((depth, pieces + 1)),
            dma((2, pieces)),
            dma((2, pieces)),
        ],
        compiler_params=pltpu.CompilerParams(
            collective_id=number, has_side_effects=True, vmem_limit_bytes=60 * 2**20
        ),
        name=f"slab_{high}",
    )(*scalars, turn, volume)


def swapped(value, axis, mask):
    pairs = [(source, source ^ mask) for source in range(lax.axis_size(axis))]
    return lax.ppermute(value, axis, pairs)


def classes_of(slab):
    top = -(-slab * RIM // GROUP) * GROUP
    rough = {int(slab * f) // GROUP * GROUP for f in (3, 4, 5, 6)}
    return sorted({h for h in rough if h >= 2 * GROUP} | {top})


def per_device(volume, shear_rows, shear_cols, warp_cols, warp_rows):
    channels, slab, rows, cols = volume.shape
    depth = lax.axis_size("depth")
    n_rows = lax.axis_size("rows")

    n_up = jnp.maximum(0, shear_rows + 1)
    n_dn = jnp.maximum(0, 1 - shear_rows)
    need = jnp.maximum(jnp.sum(n_up), jnp.sum(n_dn)).astype(jnp.int32)
    for other in [swapped(need, "depth", m) for m in range(1, depth)]:
        need = jnp.maximum(need, other)
    scalars = (shear_rows, shear_cols, warp_cols)
    sizes = classes_of(slab)
    which = sum((need > size).astype(jnp.int32) for size in sizes[:-1])
    branches = [
        functools.partial(slab_stage, size, number + 1, depth, n_rows)
        for number, size in enumerate(sizes)
    ]
    turn = warp_rows.reshape(1, -1)
    return lax.switch(which, branches, volume, scalars, turn)


def solution(mesh):
    return jax.shard_map(
        per_device,
        mesh=mesh,
        in_specs=(P(None, "depth", "rows", None), P("depth"), P("depth"), P(), P("depth")),
        out_specs=P(None, "rows", "depth"),
        check_vma=False,
    )
```

profile of v0, /device:TPU:19, one launch (start us, length us, event | category | flops | bytes accessed | tf_op | source)
XLA Modules:
  0.0 106.3 jit_solution(2057109967781740587)
XLA Ops:
  0.0 1.3 %maximum_reduce_fusion = (s32[]{:T(128)}, s32[]{:T(128)}) fusion(s32[16]{0:T(128)} %param.11), kind=kLoop, calls=%fused_computation | loop fusion | flops 94 | bytes 72 | tf_op jit(solution)/shard_map/reduce_sum | solution.py:598
  2.6 1.6 %collective-permute-start.2 = (s32[]{:T(128)}, s32[]{:T(128)}, u32[]{:S(2)}, u32[]{:S(2)}) collective-permute-start(s32[]{:T(128)} %max.20), channel_id=1, source_target_pairs={{0,24},{8,16},{16,8},{24,0},{1,25},{9,17},{17,9},{25,1},{2,26},{10... | collective-permute-start | bytes 20 | tf_op jit(solution)/shard_map/ppermute | solution.py:582
  4.2 1.9 %collective-permute-start.1 = (s32[]{:T(128)}, s32[]{:T(128)}, u32[]{:S(2)}, u32[]{:S(2)}) collective-permute-start(s32[]{:T(128)} %max.20), channel_id=1, source_target_pairs={{0,16},{8,24},{16,0},{24,8},{1,17},{9,25},{17,1},{25,9},{2,18},{10... | collective-permute-start | bytes 20 | tf_op jit(solution)/shard_map/ppermute | solution.py:582
  6.1 2.1 %collective-permute-start = (s32[]{:T(128)}, s32[]{:T(128)}, u32[]{:S(2)}, u32[]{:S(2)}) collective-permute-start(s32[]{:T(128)} %max.20), channel_id=1, source_target_pairs={{0,8},{8,0},{16,24},{24,16},{1,9},{9,1},{17,25},{25,17},{2,10},{10... | collective-permute-start | bytes 20 | tf_op jit(solution)/shard_map/ppermute | solution.py:582
  8.2 0.0 collective-permute-done
  8.9 0.0 collective-permute-done.1
  9.5 0.0 collective-permute-done.2
  10.1 95.4 %conditional.1 = (f32[4,32,1024]{2,1,0:T(8,128)S(1)}) conditional(s32[]{:T(128)} %clamp.3, (s32[16]{0:T(128)}, s32[16]{0:T(128)}, s32[256]{0:T(256)}, s32[1,1024]{1,0:T(1,128)}, bf16[4,16,32,4096]{3,2,1,0:T(8,128)(2,1)}) %tuple.32, (s32[16]{0:T(128)}, s32[16]{0:T(128)}, s32[256]{0:T(256)}, s32[1,1024]{1,0:T(1,128)}, ...), branch_computations={%region_2.0_spmd, %region_3.0_spmd, %region_4.0_spmd, %region_5.0_... | conditional | bytes 8 | solution.py:609
  10.1 94.9 %slab_80.1 = f32[4,32,1024]{2,1,0:T(8,128)S(1)} custom-call(s32[16]{0:T(128)} %get-tuple-element.71.row_s, s32[16]{0:T(128)} %get-tuple-element.72.col_s, s32[256]{0:T(256)} %get-tuple-element.73.warp_s, s32[1,1024]{1,0:T(1,128)} %get-tuple-element.74.turn_ref, bf16[4,16,32,4096]{3,2,1,0:T(8,128)(2,1)} %get-tuple-element.75.vol_hbm), custom_call_target="tpu_custom_call" | custom-call | tf_op jit(solution)/shard_map/cond/branch_2_fun/slab_80/pallas_call | solution.py:529
  105.5 0.8 copy.17
Async XLA Ops:
  2.6 6.9 %collective-permute-start.2 = (s32[]{:T(128)}, s32[]{:T(128)}, u32[]{:S(2)}, u32[]{:S(2)}) collective-permute-start(s32[]{:T(128)} %max.20), channel_id=1, source_target_pairs={{0,24},{8,16},{16,8},{24,0},{1,25},{9,17},{17,9},{25,1},{2,26},{10... | collective-permute-start | bytes 20 | tf_op jit(solution)/shard_map/ppermute | solution.py:582
  4.2 4.7 %collective-permute-start.1 = (s32[]{:T(128)}, s32[]{:T(128)}, u32[]{:S(2)}, u32[]{:S(2)}) collective-permute-start(s32[]{:T(128)} %max.20), channel_id=1, source_target_pairs={{0,16},{8,24},{16,0},{24,8},{1,17},{9,25},{17,1},{25,9},{2,18},{10... | collective-permute-start | bytes 20 | tf_op jit(solution)/shard_map/ppermute | solution.py:582
  6.1 2.1 %collective-permute-start = (s32[]{:T(128)}, s32[]{:T(128)}, u32[]{:S(2)}, u32[]{:S(2)}) collective-permute-start(s32[]{:T(128)} %max.20), channel_id=1, source_target_pairs={{0,8},{8,0},{16,24},{24,16},{1,9},{9,1},{17,25},{25,17},{2,10},{10... | collective-permute-start | bytes 20 | tf_op jit(solution)/shard_map/ppermute | solution.py:582
where the time goes:
time: 107 us; the launch traced here: 106 us
  Pallas kernels  94.9 us (89%)
  starting transfers between devices  5.62 us (5%)
  between operations  3.19 us (3%)
  other arithmetic  1.31 us (1%)
    pallas_call x1, Pallas kernels, slab_stage(): pl.pallas_call(functools.partial(slab_kernel, (depth, n_rows)), in_specs=...  94.9 us
    ppermute x3, starting transfers between devices, swapped(): return lax.ppermute(value, axis, pairs)  5.62 us
  transfers between devices with their start and end apart: 3, of which 0 were waited for; matrix products, arithmetic and copies ran while one was open for 0% of the time, Pallas kernels for 0%

commit v1 on v0

--- a/solution.py
+++ b/solution.py
@@ -9,7 +9,7 @@
 
 SHIFT = 8
 RIM = SHIFT + 1
-GROUP = 16
+GROUP = 8
 EDGE = 16
 LANES = 128
 LEAD = 16
@@ -39,7 +39,7 @@
     pick_a, pick_t, band_a, band_c, trans, t_all, ghost, acc, outb, parts, wide_ref, f_send, f_recv,
     load_sem, a_ss, a_rs, t_ss, t_rs, c_ss, c_rs, s_part, r_part, f_ss, f_rs,
 ):
-    depth, n_rows = sizes
+    depth, n_rows, wire = sizes
     chunks, channels, slab, rows, _ = vol.shape
     colours = channels - 1
     high = a_send.shape[2]
@@ -73,6 +73,10 @@
     for i in order:
         load_colour(i).start()
 
+    if wire < high:
+        for ref in (a_recv, t_recv):
+            ref[:, :, high - EDGE :] = jnp.zeros(ref.shape[:2] + (EDGE, CHUNK), BF)
+
     barrier = pltpu.get_barrier_semaphore()
     for r in (lax.rem(row + 1, n_rows), lax.rem(row + n_rows - 1, n_rows)):
         pl.semaphore_signal(barrier, inc=1, device_id=(me, r), device_id_type=MESH)
@@ -82,15 +86,16 @@
 
     def message(kind, way, i):
         source, dest, ss, rs = kind
+        part = pl.ds(0, wire if source.shape[2] == high else source.shape[2])
         return pltpu.make_async_remote_copy(
-            source.at[way, i], dest.at[way, i], ss.at[way, i], rs.at[way, i],
+            source.at[way, i, part], dest.at[way, i, part], ss.at[way, i], rs.at[way, i],
             device_id=(me, target[way]), device_id_type=MESH,
         )
 
     def lead_message(way):
         part = pl.ds(0, LANES)
         return pltpu.make_async_remote_copy(
-            a_send.at[way, chunks, :, part], a_recv.at[way, chunks, :, part],
+            a_send.at[way, chunks, pl.ds(0, wire), part], a_recv.at[way, chunks, pl.ds(0, wire), part],
             a_ss.at[way, chunks], a_rs.at[way, chunks],
             device_id=(me, target[way]), device_id_type=MESH,
         )
@@ -514,9 +519,10 @@
         sent(kind_f, h)
 
 
-def slab_stage(high, number, depth, n_rows, volume, scalars, turn):
+def slab_stage(wire, number, depth, n_rows, volume, scalars, turn):
     channels, slab, rows, cols = volume.shape
     chunks = cols // CHUNK
+    high = -(-wire // EDGE) * EDGE
     per = CHUNK // LANES
     tile = cols // depth
     flat = channels * rows
@@ -527,7 +533,7 @@
     packed = -(-channels * RIM // EDGE) * EDGE
     dma = pltpu.SemaphoreType.DMA
     return pl.pallas_call(
-        functools.partial(slab_kernel, (depth, n_rows)),
+        functools.partial(slab_kernel, (depth, n_rows, wire)),
         in_specs=[smem] * 3 + [vmem] + [pl.BlockSpec(memory_space=pl.ANY)],
         out_specs=vmem,
         out_shape=jax.ShapeDtypeStruct((channels, rows, tile), F32),
@@ -573,18 +579,62 @@
         compiler_params=pltpu.CompilerParams(
             collective_id=number, has_side_effects=True, vmem_limit_bytes=60 * 2**20
         ),
-        name=f"slab_{high}",
+        name=f"slab_{wire}",
     )(*scalars, turn, volume)
 
 
-def swapped(value, axis, mask):
-    pairs = [(source, source ^ mask) for source in range(lax.axis_size(axis))]
-    return lax.ppermute(value, axis, pairs)
+def class_kernel(sizes, depth, mine_ref, out_ref, seen, ss, rs):
+    me = lax.axis_index("depth")
+    row = lax.axis_index("rows")
+    barrier = pltpu.get_barrier_semaphore()
+    for m in range(1, depth):
+        pl.semaphore_signal(barrier, inc=1, device_id=(lax.rem(me + m, depth), row), device_id_type=MESH)
+    seen[me] = mine_ref[...]
+    pl.semaphore_wait(barrier, depth - 1)
+
+    def swap(m):
+        return pltpu.make_async_remote_copy(
+            mine_ref, seen.at[me], ss.at[m], rs.at[m],
+            device_id=(lax.rem(me + m, depth), row), device_id_type=MESH,
+        )
+
+    for m in range(1, depth):
+        swap(m).start()
+    for m in range(1, depth):
+        swap(m).wait_recv()
+    which = jnp.zeros((1, 1), F32)
+    need = jnp.zeros((1, 1), F32)
+    for d in range(depth):
+        s = seen[d].astype(F32)
+        for n in (s + 1.0, 1.0 - s):
+            need = jnp.maximum(need, jnp.sum(jnp.maximum(n, 0.0), axis=1, keepdims=True))
+    for size in sizes[:-1]:
+        which = which + jnp.where(need > size, 1.0, 0.0)
+    out_ref[0] = jnp.sum(which).astype(jnp.int32)
+    for m in range(1, depth):
+        swap(m).wait_send()
+
+
+def class_of(sizes, depth, shear_rows):
+    slab = shear_rows.shape[0]
+    return pl.pallas_call(
+        functools.partial(class_kernel, sizes, depth),
+        in_specs=[pl.BlockSpec(memory_space=pltpu.VMEM)],
+        out_specs=pl.BlockSpec(memory_space=pltpu.SMEM),
+        out_shape=jax.ShapeDtypeStruct((1,), jnp.int32),
+        scratch_shapes=[
+            pltpu.VMEM((depth, 1, slab), jnp.int32),
+            pltpu.SemaphoreType.DMA((depth,)),
+            pltpu.SemaphoreType.DMA((depth,)),
+        ],
+        compiler_params=pltpu.CompilerParams(collective_id=len(sizes) + 1, has_side_effects=True),
+        name="size_class",
+    )(shear_rows.reshape(1, slab))
 
 
 def classes_of(slab):
     top = -(-slab * RIM // GROUP) * GROUP
-    rough = {int(slab * f) // GROUP * GROUP for f in (3, 4, 5, 6)}
+    rough = {int(slab * f) // GROUP * GROUP for f in (3.5, 4, 4.5, 5.5)}
     return sorted({h for h in rough if h >= 2 * GROUP} | {top})
 
 
@@ -593,14 +643,9 @@
     depth = lax.axis_size("depth")
     n_rows = lax.axis_size("rows")
 
-    n_up = jnp.maximum(0, shear_rows + 1)
-    n_dn = jnp.maximum(0, 1 - shear_rows)
-    need = jnp.maximum(jnp.sum(n_up), jnp.sum(n_dn)).astype(jnp.int32)
-    for other in [swapped(need, "depth", m) for m in range(1, depth)]:
-        need = jnp.maximum(need, other)
     scalars = (shear_rows, shear_cols, warp_cols)
     sizes = classes_of(slab)
-    which = sum((need > size).astype(jnp.int32) for size in sizes[:-1])
+    which = class_of(sizes, depth, shear_rows)[0]
     branches = [
         functools.partial(slab_stage, size, number + 1, depth, n_rows)
         for number, size in enumerate(sizes)

time: 107 us -> 97.3 us (0.909)
  starting transfers between devices: 5.62 us -> 0 us
  between operations: 3.19 us -> 0.65 us
  other arithmetic: 1.31 us -> 0 us
    ppermute x3 -> x0, starting transfers between devices: 5.62 us -> none  [swapped(): return lax.ppermute(value, axis, pairs)]
    reduce_sum x1 -> x0, other arithmetic: 1.31 us -> none  [per_device(): need = jnp.maximum(jnp.sum(n_up), jnp.sum(n_dn)).astype(jnp.int32)]
    pallas_call x1 -> x2, Pallas kernels: 94.9 us -> 95.2 us  [the longest x1 90.2 us: slab_stage(): pl.pallas_call(functools.partial(slab_kernel, (depth, n_rows, wire)), in_...]
  transfers between devices with their start and end apart: 3 -> 0, of which waited for: 0 -> 0; matrix products, arithmetic and copies ran while one was open for 0% -> 0% of each run, Pallas kernels for 0% -> 0%
where the time goes in v1:
time: 97.3 us; the launch traced here: 97.1 us
  Pallas kernels  95.2 us (98%)
    pallas_call x1, Pallas kernels, slab_stage(): pl.pallas_call(functools.partial(slab_kernel, (depth, n_rows, wire)), in_...  90.2 us
    pallas_call x1, Pallas kernels, class_of(): pl.pallas_call(functools.partial(class_kernel, sizes, depth), in_specs=[p...  4.93 us

profile of v1, /device:TPU:19, one launch (start us, length us, event | category | flops | bytes accessed | tf_op | source)
XLA Modules:
  0.0 97.1 jit_solution(12390549484874806105)
XLA Ops:
  0.0 4.9 %size_class.1 = s32[1]{0:T(128)} custom-call(s32[1,16]{1,0:T(1,128)} %bitcast.12), custom_call_target="tpu_custom_call" | custom-call | tf_op jit(solution)/shard_map/size_class/pallas_call | solution.py:620
  5.6 90.8 %conditional.1 = (f32[4,32,1024]{2,1,0:T(8,128)S(1)}) conditional(s32[]{:T(128)} %bitcast.6, (s32[16]{0:T(128)}, s32[16]{0:T(128)}, s32[256]{0:T(256)}, s32[1024]{0:T(1024)}, bf16[4,16,32,4096]{3,2,1,0:T(8,128)(2,1)}) %tuple.20, (s32[16]{0:T(128)}, s32[16]{0:T(128)}, s32[256]{0:T(256)}, s32[1024]{0:T(1024)}, ...), branch_computations={%region_0.0_spmd, %region_1.0_spmd, %region_2.0_spmd, %region_3.0_... | conditional | bytes 8 | solution.py:654
  5.6 90.2 %slab_72.1 = f32[4,32,1024]{2,1,0:T(8,128)S(1)} custom-call(s32[16]{0:T(128)} %get-tuple-element.71.row_s, s32[16]{0:T(128)} %get-tuple-element.109.col_s, s32[256]{0:T(256)} %get-tuple-element.114.warp_s, s32[1,1024]{1,0:T(1,128)} %bitcast.9, bf16[4,16,32,4096]{3,2,1,0:T(8,128)(2,1)} %get-tuple-element.124.vol_hbm), custom_call_target="tpu_custom_call" | custom-call | tf_op jit(solution)/shard_map/cond/branch_2_fun/slab_72/pallas_call | solution.py:535
  96.3 0.8 copy.37
